TPU v7x, 32 devices: a whole 2x2x4 slice. The times are simulated.
32 devices in a mesh: req: 8 (over z, x), tp: 4 (over y, core).
Axes of the slice: x: 2, y: 2, z: 4, core: 2. Of those that a mesh axis runs over, the one named last changes fastest.
Arguments:
- tokens: bfloat16 [4096, 3584], P('req'), may hold values from -400 to 400, as said below
- norm_gain: float32 [3584], P(('req', 'tp')), may hold values from 0.5 to 1.5
- qkv_weight: float32 [3584, 4608], P(('req', 'tp')), may hold values from -0.09375 to 0.09375
- qkv_bias: float32 [4608], P(('req', 'tp')), may hold values from -48 to 48
- lengths: int32 [8, 4], P('req'), may hold values from 1 to 256, 512 in all within a row
Outputs:
- context: bfloat16 [4096, 3584], P('req', 'tp')
Inputs may be any that keep to these rules, and one draw needn't show every extreme that they name: `tokens`: hidden states of order one to some hundreds. Each replica's tenant lengths sum to 512, the largest is exactly 256.
All inputs are finite; a program needn't handle non-finite values.
Results may differ from a plain program's by a relative error of at most 0.009.
The roundings to bfloat16 on the way count: a program that leaves them out, or rounds other values in their place, can miss the bound.
Values may be sent and summed in bfloat16 or wider, within the bound.
A program may use at most 128 MiB of HBM per device.

v0:
```python
import math
import jax
import jax.numpy as jnp
from jax import lax
from jax.sharding import PartitionSpec as P

HEAD_DIM = 128
SINKS = 4
GROUP = 7
WINDOW = 160


def normalize(values, gain):
    wide = values.astype(jnp.float32)
    meansq = jnp.mean(wide * wide, axis=-1, keepdims=True)
    return (wide * lax.rsqrt(meansq + 1e-06) * gain.astype(jnp.float32)).astype(jnp.bfloat16)


def positions(lens, count):
    index = jnp.arange(count, dtype=jnp.int32)
    ends = jnp.cumsum(lens)
    after = index[:, None] >= ends[None, :]
    tenant = jnp.sum(after.astype(jnp.int32), axis=1)
    start = jnp.sum(jnp.where(after, lens[None, :], 0), axis=1)
    return (tenant, index - start)


def rotate(values, pos):
    half = HEAD_DIM // 2
    freqs = jnp.exp(-(jnp.arange(half, dtype=jnp.float32) * 2.0 / HEAD_DIM) * math.log(1000000.0))
    angle = pos.astype(jnp.float32)[:, None] * freqs[None, :]
    cosine = jnp.concatenate([jnp.cos(angle), jnp.cos(angle)], axis=-1)
    sine = jnp.concatenate([jnp.sin(angle), jnp.sin(angle)], axis=-1)
    shape = (values.shape[0],) + (1,) * (values.ndim - 2) + (HEAD_DIM,)
    cosine = cosine.reshape(shape)
    sine = sine.reshape(shape)
    turned = jnp.concatenate([-values[..., half:], values[..., :half]], axis=-1)
    return values * cosine + turned * sine


def attend(joined, tenant, pos):
    count = joined.shape[0]
    blocks = joined.reshape(count, -1, GROUP + 2, HEAD_DIM)
    query = rotate(blocks[:, :, :GROUP], pos).astype(jnp.bfloat16)
    key_part = rotate(blocks[:, :, GROUP], pos).astype(jnp.bfloat16)
    value_part = blocks[:, :, GROUP + 1].astype(jnp.bfloat16)
    scores = jnp.einsum(
        "qghd,kgd->ghqk", query, key_part, preferred_element_type=jnp.float32
    ) / math.sqrt(HEAD_DIM)
    same = tenant[:, None] == tenant[None, :]
    causal = pos[None, :] <= pos[:, None]
    near = jnp.logical_or(pos[:, None] - pos[None, :] < WINDOW, pos[None, :] < SINKS)
    allowed = jnp.logical_and(jnp.logical_and(same, causal), near)
    scores = jnp.where(allowed[None, None], scores, -1e30)
    peak = jnp.max(scores, axis=-1, keepdims=True)
    expo = jnp.where(allowed[None, None], jnp.exp(scores - peak), 0.0)
    weights = (expo / jnp.sum(expo, axis=-1, keepdims=True)).astype(jnp.bfloat16)
    mixed = jnp.einsum("ghqk,kgd->qghd", weights, value_part, preferred_element_type=jnp.float32)
    return mixed.reshape(count, -1).astype(jnp.bfloat16)


def shards(tokens, norm_gain, qkv_weight, qkv_bias, lengths):
    tp_count = lax.axis_size("tp")
    req_count = lax.axis_size("req")
    tp_place = lax.axis_index("tp")
    gain_full, bias_full = (
        lax.all_gather(norm_gain.astype(jnp.bfloat16), ("req", "tp"), axis=0, tiled=True),
        lax.all_gather(qkv_bias.astype(jnp.bfloat16), ("req", "tp"), axis=0, tiled=True),
    )
    width = bias_full.shape[0] // tp_count
    bias_block = lax.dynamic_slice_in_dim(bias_full, tp_place * width, width).astype(jnp.float32)
    normed = normalize(tokens, gain_full)
    weight_b = qkv_weight.astype(jnp.bfloat16)
    count = tokens.shape[0]
    gathered = lax.all_gather(weight_b, "req", axis=0, tiled=True)
    regrouped = lax.all_to_all(gathered, "tp", split_axis=1, concat_axis=0, tiled=True)
    shard_rows = weight_b.shape[0]
    reordered = (
        normed.reshape(count, req_count, tp_count, shard_rows)
        .transpose(0, 2, 1, 3)
        .reshape(count, -1)
    )
    joined = jnp.dot(reordered, regrouped, preferred_element_type=jnp.float32)
    joined = joined + bias_block[None, :]
    tenant, pos = positions(lengths[0], count)
    return attend(joined, tenant, pos)


def solution(mesh):
    placed = (
        P("req", None),
        P(("req", "tp")),
        P(("req", "tp"), None),
        P(("req", "tp")),
        P("req", None),
    )
    return jax.shard_map(
        shards, mesh=mesh, in_specs=placed, out_specs=P("req", "tp"), check_vma=False
    )
```

profile of v0, /device:TPU:0, one launch (start us, length us, event | category | flops | bytes accessed | tf_op | source)
XLA Modules:
  0.0 330.9 jit_solution(9403856503985649453)
XLA Ops:
  6.5 0.0 all-gather.2.cloned.1.call-start
  6.5 2.7 convert_element_type.70
  9.3 0.0 all-gather.2.cloned.1.call-update
  9.3 126.2 %all-gather.2.cloned.1.call-done = bf16[896,4608]{1,0:T(8,128)(2,1)} async-done(((bf16[112,4608]{1,0:T(8,128)(2,1)}), bf16[896,4608]{1,0:T(8,128)(2,1)}) %all-gather.2.cloned.1.call-update) | async-done | bytes 8257552 | tf_op jit(solution)/shard_map/all_gather | solution.py:75
  135.5 11.4 %copy.40 = bf16[896,4608]{0,1:T(8,128)(2,1)} copy(bf16[896,4608]{1,0:T(8,128)(2,1)} %all-gather.2.cloned.1.call-done) | data formatting | bytes 16515072 | tf_op jit(solution)/shard_map/all_gather | solution.py:75
  146.9 0.0 copy-start.2
  146.9 0.0 copy-start.1
  146.9 0.0 copy-start
  146.9 5.8 %all-to-all-start = ((bf16[896,4,1152]{0,2,1:T(8,128)(2,1)}), bf16[896,4,1152]{0,2,1:T(8,128)(2,1)}, u32[]{:S(2)}, u32[]{:S(2)}) async-start(bf16[896,4,1152]{0,2,1:T(8,128)(2,1)} %bitcast.65), calls=%async_computation | async-start | bytes 16515072 | tf_op jit(solution)/shard_map/all_to_all | solution.py:76
  152.7 0.0 copy-done.2
  152.7 0.0 copy-done.1
  152.7 0.0 copy-done
  152.7 0.2 reduce-window.8
  152.9 0.2 dynamic-update-slice
  153.1 0.2 dynamic-update-slice.1
  153.3 122.7 %all-reduce.2 = (bf16[3584]{0:T(1024)(128)(2,1)S(1)}, bf16[4608]{0:T(1024)(128)(2,1)S(1)}) all-reduce(bf16[3584]{0:T(1024)(128)(2,1)S(1)} %dynamic-update-slice, bf16[4608]{0:T(1024)(128)(2,1)S(1)} %dynamic-update-slice.1), channel_id=1, replica_groups=mesh['req'=8,'tp'=4] {'req','tp'}, use_global_device_ids=true, to_apply=%add | all-reduce | flops 8192 | bytes 32768
  276.0 5.9 %copy.38 = bf16[512,3584]{0,1:T(8,128)(2,1)} copy(bf16[512,3584]{1,0:T(8,128)(2,1)} %param.5) | data formatting | bytes 7340032 | tf_op args[0]
  282.0 2.9 fusion
  284.9 3.1 fusion.2
  288.0 2.0 copy.39
  290.0 0.1 dynamic-slice_convert_fusion
  290.1 0.1 convert_reduce_fusion
  290.2 0.5 fusion.27
  290.7 0.1 pad_maximum_fusion
  290.8 0.5 multiply_cosine_fusion.1
  291.3 0.4 fusion.14
  291.8 0.0 all-to-all-done
  291.8 11.5 %copy.41 = bf16[4,896,1152]{2,1,0:T(8,128)(2,1)} copy(bf16[4,896,1152]{1,2,0:T(8,128)(2,1)} %bitcast.4) | data formatting | bytes 16515072 | tf_op jit(solution)/shard_map/all_to_all | solution.py:76
  303.3 10.8 %convolution_add_fusion = f32[512,1152]{1,0:T(8,128)} fusion(bf16[512,3584]{0,1:T(8,128)(2,1)} %bitcast.72, bf16[3584,1152]{1,0:T(8,128)(2,1)} %bitcast.71, f32[1152]{0:T(1024)S(1)} %dynamic-slice_convert_fusion), kind=kOutput, calls=%fused_computation.13 | convolution fusion | flops 4228448256 | bytes 14291456 | tf_op jit(solution)/shard_map/dot_general | solution.py:83
  314.1 2.2 copy.42
  316.4 0.2 slice_negate_fusion
  316.6 1.7 fusion.3
  318.3 1.8 fusion.4
  320.1 2.7 fusion.10
  322.7 1.3 copy.46
  (11 shorter events, 0.1 us)
Async XLA Ops:
  6.5 128.9 %all-gather.2.cloned.1.call-start = ((), (), s32[]{:S(2)}) async-start(), calls=%async_computation.1 | async-start | bytes 9289728 | tf_op jit(solution)/shard_map/all_gather | solution.py:75
  146.9 5.8 %copy-start.2 = (f32[112]{0:T(128)S(1)}, f32[112]{0:T(128)}, u32[]{:S(2)}) copy-start(f32[112]{0:T(128)} %param.6) | copy-start | bytes 1348
  146.9 5.8 %copy-start.1 = (f32[144]{0:T(256)S(1)}, f32[144]{0:T(256)}, u32[]{:S(2)}) copy-start(f32[144]{0:T(256)} %param.8) | copy-start | bytes 1732
  146.9 5.8 %copy-start = (s32[1,4]{1,0:T(1,128)S(1)}, s32[1,4]{1,0:T(1,128)}, u32[]{:S(2)}) copy-start(s32[1,4]{1,0:T(1,128)} %param.9) | copy-start | bytes 52
  146.9 144.8 %all-to-all-start = ((bf16[896,4,1152]{0,2,1:T(8,128)(2,1)}), bf16[896,4,1152]{0,2,1:T(8,128)(2,1)}, u32[]{:S(2)}, u32[]{:S(2)}) async-start(bf16[896,4,1152]{0,2,1:T(8,128)(2,1)} %bitcast.65), calls=%async_computation | async-start | bytes 16515072 | tf_op jit(solution)/shard_map/all_to_all | solution.py:76
Sparse Core Ops, SparseCore 0:
  9.5 125.8 all-gather.1
where the time goes:
time: 332 us; the launch traced here: 331 us
  waiting for transfers between devices  126 us (38%)
  blocking collectives  123 us (37%)
  local copies, waits for them, and re-layouts  34.9 us (11%)
  matrix products  15.2 us (5%)
  between operations  13.6 us (4%)
  other arithmetic  12.6 us (4%)
  starting transfers between devices  5.76 us (2%)
    all_gather x1, waiting for transfers between devices, shards(): gathered = lax.all_gather(weight_b, 'req', axis=0, tiled=True)  126 us
    unnamed x1, blocking collectives  123 us
    all_to_all x1, local copies, waits for them, and re-layouts, shards(): lax.all_to_all(gathered, 'tp', split_axis=1, concat_axis=0, tiled=True)  11.5 us
    all_gather x1, local copies, waits for them, and re-layouts, shards(): gathered = lax.all_gather(weight_b, 'req', axis=0, tiled=True)  11.4 us
    dot_general x1, matrix products, shards(): joined = jnp.dot(reordered, regrouped, preferred_element_type=jnp.float32)  10.8 us
  transfers between devices with their start and end apart: 2, of which 1 were waited for; matrix products, arithmetic and copies ran while one was open for 5% of the time, Pallas kernels for 0%

commit v1 on v0

--- a/solution.py
+++ b/solution.py
@@ -8,6 +8,28 @@
 SINKS = 4
 GROUP = 7
 WINDOW = 160
+
+
+def in_order(blocks, dim):
+    blocks = jnp.moveaxis(blocks, 0, dim)
+    lengths = blocks.shape
+    return blocks.reshape(*lengths[:dim], lengths[dim] * lengths[dim + 1], *lengths[dim + 2 :])
+
+
+def gather_around(shard, axis, dim):
+    devices = lax.axis_size(axis)
+    pairs = [(i, (i + 1) % devices) for i in range(devices)]
+    back = [(b, a) for a, b in pairs]
+    lower, upper = ([], [])
+    for turn in range(devices - 1):
+        if turn % 2 == 0:
+            lower.append(lax.ppermute(lower[-1] if lower else shard, axis, pairs))
+        else:
+            upper.append(lax.ppermute(upper[-1] if upper else shard, axis, back))
+    blocks = jnp.stack([*lower[::-1], shard, *upper])
+    shift = lax.axis_index(axis) - len(lower)
+    blocks = blocks[(jnp.arange(devices) - shift) % devices]
+    return in_order(blocks, dim)
 
 
 def normalize(values, gain):
@@ -72,7 +94,7 @@
     normed = normalize(tokens, gain_full)
     weight_b = qkv_weight.astype(jnp.bfloat16)
     count = tokens.shape[0]
-    gathered = lax.all_gather(weight_b, "req", axis=0, tiled=True)
+    gathered = gather_around(weight_b, "req", 0)
     regrouped = lax.all_to_all(gathered, "tp", split_axis=1, concat_axis=0, tiled=True)
     shard_rows = weight_b.shape[0]
     reordered = (

time: 332 us -> 376 us (1.13)
  starting transfers between devices: 5.76 us -> 66.3 us
  waiting for transfers between devices: 126 us -> 103 us
  local copies, waits for them, and re-layouts: 34.9 us -> 52.7 us
  between operations: 13.6 us -> 0.21 us
    all_gather x1 -> x0, waiting for transfers between devices: 126 us -> none  [shards(): gathered = lax.all_gather(weight_b, 'req', axis=0, tiled=True)]
    ppermute x0 -> x7, waiting for transfers between devices: none -> 103 us  [the longest x4 103 us: gather_around(): lower.append(lax.ppermute(lower[-1] if lower else shard, axis, pairs))]
    ppermute x0 -> x7, starting transfers between devices: none -> 60.5 us  [the longest x3 52.4 us: gather_around(): upper.append(lax.ppermute(upper[-1] if upper else shard, axis, back))]
    unnamed x11 -> x21, local copies, waits for them, and re-layouts: 6.38 us -> 18.9 us
    all_gather x1 -> x0, local copies, waits for them, and re-layouts: 11.4 us -> none  [shards(): gathered = lax.all_gather(weight_b, 'req', axis=0, tiled=True)]
    gather x0 -> x1, local copies, waits for them, and re-layouts: none -> 7.97 us  [gather_around(): blocks = blocks[(jnp.arange(devices) - shift) % devices]]
    all_to_all x1 -> x2, local copies, waits for them, and re-layouts: 11.5 us -> 19.2 us  [shards(): lax.all_to_all(gathered, 'tp', split_axis=1, concat_axis=0, tiled=True)]
  transfers between devices with their start and end apart: 2 -> 8, of which waited for: 1 -> 4; matrix products, arithmetic and copies ran while one was open for 5% -> 8% of each run, Pallas kernels for 0% -> 0%
where the time goes in v1:
time: 376 us; the launch traced here: 375 us
  blocking collectives  125 us (33%)
  waiting for transfers between devices  103 us (27%)
  starting transfers between devices  66.3 us (18%)
  local copies, waits for them, and re-layouts  52.7 us (14%)
  matrix products  15.2 us (4%)
  other arithmetic  12.8 us (3%)
    unnamed x1, blocking collectives  125 us
    ppermute x4, waiting for transfers between devices, gather_around(): lower.append(lax.ppermute(lower[-1] if lower else shard, axis, pairs))  103 us
    ppermute x3, starting transfers between devices, gather_around(): upper.append(lax.ppermute(upper[-1] if upper else shard, axis, back))  52.4 us
    all_to_all x2, local copies, waits for them, and re-layouts, shards(): lax.all_to_all(gathered, 'tp', split_axis=1, concat_axis=0, tiled=True)  19.2 us
    unnamed x21, local copies, waits for them, and re-layouts  18.9 us
    dot_general x1, matrix products, shards(): joined = jnp.dot(reordered, regrouped, preferred_element_type=jnp.float32)  10.9 us
    ppermute x4, starting transfers between devices, gather_around(): lower.append(lax.ppermute(lower[-1] if lower else shard, axis, pairs))  8.06 us
    gather x1, local copies, waits for them, and re-layouts, gather_around(): blocks = blocks[(jnp.arange(devices) - shift) % devices]  7.97 us
  transfers between devices with their start and end apart: 8, of which 4 were waited for; matrix products, arithmetic and copies ran while one was open for 8% of the time, Pallas kernels for 0%

profile of v1, /device:TPU:0, one launch (start us, length us, event | category | flops | bytes accessed | tf_op | source)
XLA Modules:
  0.0 374.9 jit_solution(3140960782152446073)
XLA Ops:
  0.0 1.8 convert_element_type.70
  1.8 3.0 collective-permute-start
  4.8 25.8 %collective-permute-done = bf16[112,4608]{1,0:T(8,128)(2,1)S(1)} collective-permute-done((bf16[112,4608]{1,0:T(8,128)(2,1)S(1)}, bf16[112,4608]{1,0:T(8,128)(2,1)S(1)}, u32[]{:S(2)}, u32[]{:S(2)}) %collective-permute-start) | collective-permute-done | bytes 1032224 | tf_op jit(solution)/shard_map/ppermute | solution.py:26
  30.7 0.0 collective-permute-start.1
  30.7 4.7 %collective-permute-start.4 = (bf16[112,4608]{1,0:T(8,128)(2,1)S(1)}, bf16[112,4608]{1,0:T(8,128)(2,1)}, u32[]{:S(2)}, u32[]{:S(2)}) collective-permute-start(bf16[112,4608]{1,0:T(8,128)(2,1)S(1)} %convert_element_type.70), channel_id=1, source_target_pairs={{4,0},{8,4},{12,8},{16,12},{20,16},{24,20},{28,24},{0,28},{5,1},{9... | collective-permute-start | bytes 3096584 | tf_op jit(solution)/shard_map/ppermute | solution.py:28
  35.4 39.2 %collective-permute-done.1 = bf16[112,4608]{1,0:T(8,128)(2,1)S(1)} collective-permute-done((bf16[112,4608]{1,0:T(8,128)(2,1)S(1)}, bf16[112,4608]{1,0:T(8,128)(2,1)S(1)}, u32[]{:S(2)}, u32[]{:S(2)}) %collective-permute-start.1) | collective-permute-done | bytes 1032224 | tf_op jit(solution)/shard_map/ppermute | solution.py:26
  74.6 2.5 collective-permute-start.2
  77.1 0.0 collective-permute-done.4
  77.1 23.1 %collective-permute-start.5 = (bf16[112,4608]{1,0:T(8,128)(2,1)}, bf16[112,4608]{1,0:T(8,128)(2,1)}, u32[]{:S(2)}, u32[]{:S(2)}) collective-permute-start(bf16[112,4608]{1,0:T(8,128)(2,1)} %collective-permute-done.4), channel_id=1, source_target_pairs={{4,0},{8,4},{12,8},{16,12},{20,16},{24,20},{28,24},{0,28},{5,1},{9... | collective-permute-start | bytes 3096584 | tf_op jit(solution)/shard_map/ppermute | solution.py:28
  100.2 20.0 %collective-permute-done.2 = bf16[112,4608]{1,0:T(8,128)(2,1)} collective-permute-done((bf16[112,4608]{1,0:T(8,128)(2,1)S(1)}, bf16[112,4608]{1,0:T(8,128)(2,1)}, u32[]{:S(2)}, u32[]{:S(2)}) %collective-permute-start.2) | collective-permute-done | bytes 1032224 | tf_op jit(solution)/shard_map/ppermute | solution.py:26
  120.2 2.6 collective-permute-start.3
  122.8 24.6 %collective-permute-start.6 = (bf16[112,4608]{1,0:T(8,128)(2,1)}, bf16[112,4608]{1,0:T(8,128)(2,1)S(1)}, u32[]{:S(2)}, u32[]{:S(2)}) collective-permute-start(bf16[112,4608]{1,0:T(8,128)(2,1)} %collective-permute-done.5), channel_id=1, source_target_pairs={{4,0},{8,4},{12,8},{16,12},{20,16},{24,20},{28,24},{0,28},{5,1},{9... | collective-permute-start | bytes 3096584 | tf_op jit(solution)/shard_map/ppermute | solution.py:28
  147.5 17.9 %collective-permute-done.3 = bf16[112,4608]{1,0:T(8,128)(2,1)} collective-permute-done((bf16[112,4608]{1,0:T(8,128)(2,1)}, bf16[112,4608]{1,0:T(8,128)(2,1)}, u32[]{:S(2)}, u32[]{:S(2)}) %collective-permute-start.3) | collective-permute-done | bytes 1032224 | tf_op jit(solution)/shard_map/ppermute | solution.py:26
  165.4 2.3 bitcast_dynamic-update-slice_fusion.7
  167.6 2.3 bitcast_dynamic-update-slice_fusion.6
  169.9 2.3 bitcast_dynamic-update-slice_fusion.5
  172.2 1.0 bitcast_dynamic-update-slice_fusion.4
  173.2 1.1 bitcast_dynamic-update-slice_fusion.3
  174.3 2.3 bitcast_dynamic-update-slice_fusion.2
  176.6 2.3 bitcast_dynamic-update-slice_fusion.1
  178.9 0.0 collective-permute-done.6
  178.9 1.0 bitcast_dynamic-update-slice_fusion
  179.9 8.0 %gather_fusion = bf16[8,112,4608]{2,1,0:T(8,128)(2,1)} fusion(bf16[8,112,4608]{2,1,0:T(8,128)(2,1)} %bitcast_dynamic-update-slice_fusion, s32[1024]{0:T(1024)S(1)} %pad_clamp_fusion), kind=kCustom, calls=%fused_computation | custom fusion | bytes 16515104 | tf_op jit(solution)/shard_map/gather | solution.py:31
  187.9 11.7 %all_to_all.14 = bf16[896,4,1152]{2,1,0:T(4,128)(2,1)} reshape(bf16[8,112,4608]{2,1,0:T(8,128)(2,1)} %gather_fusion) | data formatting | bytes 16515072 | tf_op jit(solution)/shard_map/all_to_all | solution.py:98
  199.5 7.6 %copy.38 = bf16[896,4,1152]{2,0,1:T(8,128)(2,1)} copy(bf16[896,4,1152]{2,1,0:T(4,128)(2,1)} %all_to_all.14) | data formatting | bytes 16515072 | tf_op jit(solution)/shard_map/all_to_all | solution.py:98
  207.1 5.8 %all-to-all-start = ((bf16[896,4,1152]{2,0,1:T(8,128)(2,1)}), bf16[896,4,1152]{2,0,1:T(8,128)(2,1)}, u32[]{:S(2)}, u32[]{:S(2)}) async-start(bf16[896,4,1152]{2,0,1:T(8,128)(2,1)} %copy.38), calls=%async_computation | async-start | bytes 16515072 | tf_op jit(solution)/shard_map/all_to_all | solution.py:98
  212.9 0.2 dynamic-update-slice.1
  213.2 0.2 dynamic-update-slice
  213.4 124.7 %all-reduce.2 = (bf16[3584]{0:T(1024)(128)(2,1)S(1)}, bf16[4608]{0:T(1024)(128)(2,1)S(1)}) all-reduce(bf16[3584]{0:T(1024)(128)(2,1)S(1)} %dynamic-update-slice, bf16[4608]{0:T(1024)(128)(2,1)S(1)} %dynamic-update-slice.1), channel_id=1, replica_groups=mesh['req'=8,'tp'=4] {'req','tp'}, use_global_device_ids=true, to_apply=%add | all-reduce | flops 8192 | bytes 32768
  338.1 6.0 %copy.36 = bf16[512,3584]{0,1:T(8,128)(2,1)} copy(bf16[512,3584]{1,0:T(8,128)(2,1)} %param.5) | data formatting | bytes 7340032 | tf_op args[0]
  344.1 2.9 fusion
  347.0 3.1 fusion.2
  350.1 2.0 copy.37
  352.1 0.2 reduce-window.8
  352.3 0.1 dynamic-slice_convert_fusion
  352.4 0.1 convert_reduce_fusion
  352.5 0.5 fusion.27
  353.1 0.1 pad_maximum_fusion
  353.1 0.5 multiply_cosine_fusion.1
  353.6 0.4 fusion.14
  354.1 0.0 all-to-all-done
  354.1 10.9 %convolution_add_fusion = f32[512,1152]{1,0:T(8,128)} fusion(bf16[512,3584]{0,1:T(8,128)(2,1)} %bitcast.88, bf16[3584,1152]{1,0:T(8,128)(2,1)} %bitcast.13, f32[1152]{0:T(1024)S(1)} %dynamic-slice_convert_fusion), kind=kOutput, calls=%fused_computation.14 | convolution fusion | flops 4228448256 | bytes 14291456 | tf_op jit(solution)/shard_map/dot_general | solution.py:105
  365.0 2.3 copy.39
  367.2 0.2 slice_negate_fusion
  367.5 1.6 fusion.3
  369.1 1.8 fusion.4
  370.9 2.7 fusion.10
  373.6 1.3 copy.43
  (24 shorter events, 0.1 us)
Async XLA Ops:
  0.0 173.2 %copy-start = (f32[112,4608]{1,0:T(8,128)S(1)}, f32[112,4608]{1,0:T(8,128)}, u32[]{:S(2)}) copy-start(f32[112,4608]{1,0:T(8,128)} %param.7) | copy-start | bytes 6193156
  1.8 28.8 %collective-permute-start = (bf16[112,4608]{1,0:T(8,128)(2,1)S(1)}, bf16[112,4608]{1,0:T(8,128)(2,1)S(1)}, u32[]{:S(2)}, u32[]{:S(2)}) collective-permute-start(bf16[112,4608]{1,0:T(8,128)(2,1)S(1)} %convert_element_type.70), channel_id=1, source_target_pairs={{0,4},{4,8},{8,12},{12,16},{16,20},{20,24},{24,28},{28,0},{1,5},{5... | collective-permute-start | bytes 3096584 | tf_op jit(solution)/shard_map/ppermute | solution.py:26
  30.7 43.9 %collective-permute-start.1 = (bf16[112,4608]{1,0:T(8,128)(2,1)S(1)}, bf16[112,4608]{1,0:T(8,128)(2,1)S(1)}, u32[]{:S(2)}, u32[]{:S(2)}) collective-permute-start(bf16[112,4608]{1,0:T(8,128)(2,1)S(1)} %collective-permute-done), channel_id=1, source_target_pairs={{0,4},{4,8},{8,12},{12,16},{16,20},{20,24},{24,28},{28,0},{1,5},{5... | collective-permute-start | bytes 3096584 | tf_op jit(solution)/shard_map/ppermute | solution.py:26
  30.7 46.4 %collective-permute-start.4 = (bf16[112,4608]{1,0:T(8,128)(2,1)S(1)}, bf16[112,4608]{1,0:T(8,128)(2,1)}, u32[]{:S(2)}, u32[]{:S(2)}) collective-permute-start(bf16[112,4608]{1,0:T(8,128)(2,1)S(1)} %convert_element_type.70), channel_id=1, source_target_pairs={{4,0},{8,4},{12,8},{16,12},{20,16},{24,20},{28,24},{0,28},{5,1},{9... | collective-permute-start | bytes 3096584 | tf_op jit(solution)/shard_map/ppermute | solution.py:28
  74.6 2.5 copy-start.1
  74.6 45.6 %collective-permute-start.2 = (bf16[112,4608]{1,0:T(8,128)(2,1)S(1)}, bf16[112,4608]{1,0:T(8,128)(2,1)}, u32[]{:S(2)}, u32[]{:S(2)}) collective-permute-start(bf16[112,4608]{1,0:T(8,128)(2,1)S(1)} %collective-permute-done.1), channel_id=1, source_target_pairs={{0,4},{4,8},{8,12},{12,16},{16,20},{20,24},{24,28},{28,0},{1,5},{5... | collective-permute-start | bytes 3096584 | tf_op jit(solution)/shard_map/ppermute | solution.py:26
  77.1 45.8 %collective-permute-start.5 = (bf16[112,4608]{1,0:T(8,128)(2,1)}, bf16[112,4608]{1,0:T(8,128)(2,1)}, u32[]{:S(2)}, u32[]{:S(2)}) collective-permute-start(bf16[112,4608]{1,0:T(8,128)(2,1)} %collective-permute-done.4), channel_id=1, source_target_pairs={{4,0},{8,4},{12,8},{16,12},{20,16},{24,20},{28,24},{0,28},{5,1},{9... | collective-permute-start | bytes 3096584 | tf_op jit(solution)/shard_map/ppermute | solution.py:28
  120.2 45.1 %collective-permute-start.3 = (bf16[112,4608]{1,0:T(8,128)(2,1)}, bf16[112,4608]{1,0:T(8,128)(2,1)}, u32[]{:S(2)}, u32[]{:S(2)}) collective-permute-start(bf16[112,4608]{1,0:T(8,128)(2,1)} %collective-permute-done.2), channel_id=1, source_target_pairs={{0,4},{4,8},{8,12},{12,16},{16,20},{20,24},{24,28},{28,0},{1,5},{5... | collective-permute-start | bytes 3096584 | tf_op jit(solution)/shard_map/ppermute | solution.py:26
  122.8 56.0 %collective-permute-start.6 = (bf16[112,4608]{1,0:T(8,128)(2,1)}, bf16[112,4608]{1,0:T(8,128)(2,1)S(1)}, u32[]{:S(2)}, u32[]{:S(2)}) collective-permute-start(bf16[112,4608]{1,0:T(8,128)(2,1)} %collective-permute-done.5), channel_id=1, source_target_pairs={{4,0},{8,4},{12,8},{16,12},{20,16},{24,20},{28,24},{0,28},{5,1},{9... | collective-permute-start | bytes 3096584 | tf_op jit(solution)/shard_map/ppermute | solution.py:28
  207.1 5.8 %copy-start.3 = (f32[144]{0:T(256)S(1)}, f32[144]{0:T(256)}, u32[]{:S(2)}) copy-start(f32[144]{0:T(256)} %param.8) | copy-start | bytes 1732
  207.1 5.8 %copy-start.4 = (f32[112]{0:T(128)S(1)}, f32[112]{0:T(128)}, u32[]{:S(2)}) copy-start(f32[112]{0:T(128)} %param.6) | copy-start | bytes 1348
  207.1 147.0 %all-to-all-start = ((bf16[896,4,1152]{2,0,1:T(8,128)(2,1)}), bf16[896,4,1152]{2,0,1:T(8,128)(2,1)}, u32[]{:S(2)}, u32[]{:S(2)}) async-start(bf16[896,4,1152]{2,0,1:T(8,128)(2,1)} %copy.38), calls=%async_computation | async-start | bytes 16515072 | tf_op jit(solution)/shard_map/all_to_all | solution.py:98
  347.0 5.2 %copy-start.2 = (s32[1,4]{1,0:T(1,128)S(1)}, s32[1,4]{1,0:T(1,128)}, u32[]{:S(2)}) copy-start(s32[1,4]{1,0:T(1,128)} %param.9) | copy-start | bytes 52
